TPU v7x, 32 devices: a whole 2x2x4 slice. The times are simulated.
32 devices in a mesh: row: 8 (over y, x, core), ka: 4 (over z).
Axes of the slice: x: 2, y: 2, z: 4, core: 2. Of those that a mesh axis runs over, the one named last changes fastest.
Arguments:
- pair_rep: bfloat16 [32, 32, 128], P('row', 'ka'), may hold values from -6 to 6
- in_weights: bfloat16 [2, 128, 512], replicated, may hold values from -0.5 to 0.5
- gate_weights: bfloat16 [2, 128, 128], replicated, may hold values from -0.5 to 0.5
- out_weights: bfloat16 [2, 128, 128], replicated, may hold values from -0.5 to 0.5
Outputs:
- refined: bfloat16 [32, 32, 128], P('row', 'ka')
All inputs are finite; a program needn't handle non-finite values.
Results may differ from a plain program's by a relative error of at most 0.015.
Values may be sent and summed in bfloat16 or wider, within the bound.
A program may use at most 64 MiB of HBM per device.

v0:
```python
import jax
import jax.numpy as jnp
from jax import lax
from jax.sharding import PartitionSpec as P

EPSILON = 1e-05


def normalize(values):
    values = values.astype(jnp.float32)
    centre = jnp.mean(values, axis=-1, keepdims=True)
    shifted = values - centre
    spread = jnp.mean(shifted * shifted, axis=-1, keepdims=True)
    return shifted * lax.rsqrt(spread + EPSILON)


def flatten_normed(blocks):
    normed = normalize(blocks).astype(jnp.bfloat16)
    return normed.reshape(-1, blocks.shape[-1])


def operands(flattened, weights, shape):
    columns = weights.shape[1] // 4
    projected = jnp.dot(flattened, weights, preferred_element_type=jnp.float32)
    left_rows = (
        jax.nn.sigmoid(projected[:, :columns]) * projected[:, columns : 2 * columns]
    ).astype(jnp.bfloat16)
    right_rows = (
        jax.nn.sigmoid(projected[:, 2 * columns : 3 * columns]) * projected[:, 3 * columns :]
    ).astype(jnp.bfloat16)
    return (
        left_rows.reshape(shape[0], shape[1], columns),
        right_rows.reshape(shape[0], shape[1], columns),
    )


def gates(flattened, weights, shape):
    gating = jax.nn.sigmoid(jnp.dot(flattened, weights, preferred_element_type=jnp.float32))
    return gating.reshape(shape[0], shape[1], weights.shape[1])


def triangle(left_rows, right_rows):
    partial_value = jnp.einsum(
        "ikh,jkh->ijh",
        left_rows,
        lax.all_gather(right_rows, "row", axis=0, tiled=True),
        preferred_element_type=jnp.float32,
    )
    return lax.psum_scatter(
        partial_value.astype(jnp.bfloat16), "ka", scatter_dimension=1, tiled=True
    ).astype(jnp.float32)


def finish(state, gating, product, weights):
    squeezed = normalize(product).astype(jnp.bfloat16).reshape(-1, product.shape[-1])
    update = jnp.dot(squeezed, weights, preferred_element_type=jnp.float32).reshape(gating.shape)
    return (state.astype(jnp.float32) + gating * update).astype(jnp.bfloat16)


def per_device(pair_rep, in_weights, gate_weights, out_weights):
    shape = pair_rep.shape
    flattened = flatten_normed(pair_rep)
    left_rows, right_rows = operands(flattened, in_weights[0], shape)
    gating = gates(flattened, gate_weights[0], shape)
    middle = finish(pair_rep, gating, triangle(left_rows, right_rows), out_weights[0])
    arrived = lax.all_to_all(
        jnp.swapaxes(middle, 0, 1), "ka", split_axis=1, concat_axis=0, tiled=True
    )
    arrived = lax.all_to_all(arrived, "row", split_axis=0, concat_axis=1, tiled=True)
    left_far, right_far = operands(flatten_normed(arrived), in_weights[1], arrived.shape)
    gating_far = gates(flatten_normed(middle), gate_weights[1], shape)
    return finish(middle, gating_far, triangle(left_far, right_far), out_weights[1])


def solution(mesh):
    in_specs = (P("row", "ka", None), P(), P(), P())
    out_specs = P("row", "ka", None)
    return jax.shard_map(
        per_device, mesh=mesh, in_specs=in_specs, out_specs=out_specs, check_vma=False
    )
```

profile of v0, /device:TPU:0, one launch (start us, length us, event | category | flops | bytes accessed | tf_op | source)
XLA Modules:
  0.0 86.3 jit_solution(1620669610929316636)
XLA Ops:
  0.0 0.9 convert_reduce_fusion.1
  1.0 1.1 %fusion.16 = f32[32,512]{1,0:T(8,128)S(1)} fusion(bf16[2,128,512]{2,1,0:T(8,128)(2,1)} %param.5, bf16[4,8,128]{2,1,0:T(8,128)(2,1)S(1)} %copy-done.1, f32[4,8]{1,0:T(4,128)S(1)} %add_rsqrt_fusion.4, f32[4,8]{1,0:T(4,128)S(1)} %broadcast_multiply_fusion.4), kind=kOutput, calls=%fused_computation.22 | convolution fusion | flops 4210688 | bytes 205056 | tf_op jit(solution)/shard_map/dot_general | solution.py:24
  2.2 10.7 %all_gather.6 = bf16[32,8,128]{2,1,0:T(8,128)(2,1)S(1)} all-gather(bf16[4,8,128]{2,1,0:T(8,128)(2,1)S(1)} %get-tuple-element.8), channel_id=1, replica_groups=mesh['row'=8,'ka'=4] {'row'}, dimensions={0}, use_global_device_ids=true | all-gather | bytes 73728 | tf_op jit(solution)/shard_map/all_gather | solution.py:46
  12.9 1.4 %copy.65 = bf16[32,8,128]{1,0,2:T(8,128)(2,1)S(1)} copy(bf16[32,8,128]{2,1,0:T(8,128)(2,1)S(1)} %all_gather.6) | data formatting | bytes 131072 | tf_op jit(solution)/shard_map/all_gather | solution.py:46
  14.5 0.6 fusion
  15.3 19.4 %all-reduce = bf16[4,32,128]{2,0,1:T(4,128)(2,1)S(1)} all-reduce(bf16[4,32,128]{2,0,1:T(4,128)(2,1)S(1)} %copy.67), channel_id=2, replica_groups=mesh['row'=8,'ka'=4] {'ka'}, use_global_device_ids=true, to_apply=%region_2.0.clone | all-reduce | flops 16384 | bytes 65536
  34.7 0.6 copy-done.4
  35.3 0.6 dynamic-slice
  37.2 0.4 copy-done.2
  37.5 0.7 convert_reduce_fusion
  38.3 3.2 %all-to-all-start = ((bf16[8,4,128]{2,0,1:T(8,128)(2,1)}), bf16[8,4,128]{2,0,1:T(8,128)(2,1)S(1)}, u32[]{:S(2)}, u32[]{:S(2)}) async-start(bf16[8,4,128]{2,0,1:T(8,128)(2,1)} %bitcast.12), calls=%async_computation | async-start | bytes 16384 | tf_op jit(solution)/shard_map/all_to_all | solution.py:66
  41.5 0.9 %fusion.42 = f32[4,8]{1,0:T(4,128)S(1)} fusion(bf16[4,8,128]{2,1,0:T(8,128)(2,1)} %get-tuple-element.10, f32[4,8]{1,0:T(4,128)S(1)} %broadcast_multiply_fusion.3), kind=kLoop, calls=%fused_computation.58 | loop fusion | flops 16352 | bytes 8448 | tf_op jit(solution)/shard_map/reduce_sum | solution.py:13
  42.4 4.6 %all-to-all-done = bf16[8,4,128]{2,0,1:T(8,128)(2,1)S(1)} async-done(((bf16[8,4,128]{2,0,1:T(8,128)(2,1)}), bf16[8,4,128]{2,0,1:T(8,128)(2,1)S(1)}, u32[]{:S(2)}, u32[]{:S(2)}) %all-to-all-start) | async-done | bytes 8224 | tf_op jit(solution)/shard_map/all_to_all | solution.py:66
  47.1 0.6 broadcast.145
  47.7 0.7 reduce.1
  48.4 0.6 reshape.129
  49.0 3.3 %all-to-all-start.1 = ((bf16[8,2,256]{2,1,0:T(2,128)(2,1)}), bf16[8,2,256]{2,1,0:T(2,128)(2,1)S(1)}, u32[]{:S(2)}, u32[]{:S(2)}) async-start(bf16[8,2,256]{2,1,0:T(2,128)(2,1)} %reshape.129), calls=%async_computation.1 | async-start | bytes 16384 | tf_op jit(solution)/shard_map/all_to_all | solution.py:69
  52.3 0.9 %fusion.6 = f32[4,8,128]{2,1,0:T(8,128)S(1)} fusion(bf16[2,128,128]{2,1,0:T(8,128)(2,1)S(1)} %copy-done.3, bf16[4,8,128]{2,1,0:T(8,128)(2,1)} %get-tuple-element.10, f32[4,8]{1,0:T(4,128)S(1)} %add_rsqrt_fusion.3, f32[4,8]{1,0:T(4,128)S(1)} %broadcast_multiply_fusion.3), kind=kOutput, calls=%fused_computation.10 | convolution fusion | flops 1077248 | bytes 61440 | tf_op jit(solution)/shard_map/dot_general | solution.py:38
  53.2 3.7 %all-to-all-done.1 = bf16[8,2,256]{2,1,0:T(2,128)(2,1)S(1)} async-done(((bf16[8,2,256]{2,1,0:T(2,128)(2,1)}), bf16[8,2,256]{2,1,0:T(2,128)(2,1)S(1)}, u32[]{:S(2)}, u32[]{:S(2)}) %all-to-all-start.1) | async-done | bytes 8224 | tf_op jit(solution)/shard_map/all_to_all | solution.py:69
  57.5 8.3 %all_gather.7 = bf16[32,8,128]{2,1,0:T(8,128)(2,1)S(1)} all-gather(bf16[4,8,128]{2,1,0:T(8,128)(2,1)S(1)} %get-tuple-element.6), channel_id=1, replica_groups=mesh['row'=8,'ka'=4] {'row'}, dimensions={0}, use_global_device_ids=true | all-gather | bytes 73728 | tf_op jit(solution)/shard_map/all_gather | solution.py:46
  65.8 1.4 %copy.81 = bf16[32,8,128]{1,0,2:T(8,128)(2,1)S(1)} copy(bf16[32,8,128]{2,1,0:T(8,128)(2,1)S(1)} %all_gather.7) | data formatting | bytes 131072 | tf_op jit(solution)/shard_map/all_gather | solution.py:46
  67.4 0.6 fusion.1
  68.2 16.3 %all-reduce.1 = bf16[4,32,128]{2,0,1:T(4,128)(2,1)S(1)} all-reduce(bf16[4,32,128]{2,0,1:T(4,128)(2,1)S(1)} %copy.83), channel_id=3, replica_groups=mesh['row'=8,'ka'=4] {'ka'}, use_global_device_ids=true, to_apply=%region_9.0.clone | all-reduce | flops 16384 | bytes 65536
  84.8 1.4 %fusion.13 = bf16[4,8,128]{2,1,0:T(8,128)(2,1)} fusion(f32[4,8,128]{2,1,0:T(8,128)S(1)} %fusion.6, bf16[2,128,128]{2,1,0:T(8,128)(2,1)S(1)} %copy-done.2, bf16[4,8,128]{2,1,0:T(8,128)(2,1)} %get-tuple-element.10, bf16[4,8,128]{2,0,1:T(4,128)(2,1)S(1)} %fusion.39), kind=kOutput, calls=%fused_computation.19 | convolution fusion | flops 1064960 | bytes 73728 | tf_op jit(solution)/shard_map/dot_general | solution.py:56
  (38 shorter events, 2.2 us)
Async XLA Ops:
  0.0 0.9 %copy-start.1 = (bf16[4,8,128]{2,1,0:T(8,128)(2,1)S(1)}, bf16[4,8,128]{2,1,0:T(8,128)(2,1)}, u32[]{:S(2)}) copy-start(bf16[4,8,128]{2,1,0:T(8,128)(2,1)} %param.4) | copy-start | bytes 24580
  15.3 21.7 %copy-start.3 = (bf16[2,128,128]{2,1,0:T(8,128)(2,1)S(1)}, bf16[2,128,128]{2,1,0:T(8,128)(2,1)}, u32[]{:S(2)}) copy-start(bf16[2,128,128]{2,1,0:T(8,128)(2,1)} %param.6) | copy-start | bytes 196612
  34.7 0.7 copy-start.4
  36.7 0.8 copy-start.2
  37.0 20.4 %copy-start = (bf16[2,128,512]{2,1,0:T(8,128)(2,1)S(1)}, bf16[2,128,512]{2,1,0:T(8,128)(2,1)}, u32[]{:S(2)}) copy-start(bf16[2,128,512]{2,1,0:T(8,128)(2,1)} %param.5) | copy-start | bytes 786436
  38.3 8.8 %all-to-all-start = ((bf16[8,4,128]{2,0,1:T(8,128)(2,1)}), bf16[8,4,128]{2,0,1:T(8,128)(2,1)S(1)}, u32[]{:S(2)}, u32[]{:S(2)}) async-start(bf16[8,4,128]{2,0,1:T(8,128)(2,1)} %bitcast.12), calls=%async_computation | async-start | bytes 16384 | tf_op jit(solution)/shard_map/all_to_all | solution.py:66
  49.0 8.0 %all-to-all-start.1 = ((bf16[8,2,256]{2,1,0:T(2,128)(2,1)}), bf16[8,2,256]{2,1,0:T(2,128)(2,1)S(1)}, u32[]{:S(2)}, u32[]{:S(2)}) async-start(bf16[8,2,256]{2,1,0:T(2,128)(2,1)} %reshape.129), calls=%async_computation.1 | async-start | bytes 16384 | tf_op jit(solution)/shard_map/all_to_all | solution.py:69
where the time goes:
time: 86.9 us; the launch traced here: 86.3 us
  blocking collectives  54.7 us (63%)
  waiting for transfers between devices  8.39 us (10%)
  starting transfers between devices  6.58 us (8%)
  local copies, waits for them, and re-layouts  6.25 us (7%)
  matrix products  5.78 us (7%)
  other arithmetic  3.7 us (4%)
  between operations  0.88 us (1%)
    unnamed x2, blocking collectives  35.7 us
    all_gather x2, blocking collectives, triangle(): lax.all_gather(right_rows, 'row', axis=0, tiled=True)  19 us
    all_to_all x1, waiting for transfers between devices, per_device(): lax.all_to_all(jnp.swapaxes(middle, 0, 1), 'ka', split_axis=1, concat_axi...  4.65 us
    all_to_all x1, waiting for transfers between devices, per_device(): lax.all_to_all(arrived, 'row', split_axis=0, concat_axis=1, tiled=True)  3.74 us
    all_to_all x1, starting transfers between devices, per_device(): lax.all_to_all(arrived, 'row', split_axis=0, concat_axis=1, tiled=True)  3.33 us
    all_to_all x1, starting transfers between devices, per_device(): lax.all_to_all(jnp.swapaxes(middle, 0, 1), 'ka', split_axis=1, concat_axi...  3.25 us
    all_gather x2, local copies, waits for them, and re-layouts, triangle(): lax.all_gather(right_rows, 'row', axis=0, tiled=True)  2.86 us
    unnamed x13, local copies, waits for them, and re-layouts  2.22 us
  transfers between devices with their start and end apart: 2, of which 2 were waited for; matrix products, arithmetic and copies ran while one was open for 2% of the time, Pallas kernels for 0%

commit v1 on v0

--- a/solution.py
+++ b/solution.py
@@ -66,7 +66,10 @@
     arrived = lax.all_to_all(
         jnp.swapaxes(middle, 0, 1), "ka", split_axis=1, concat_axis=0, tiled=True
     )
-    arrived = lax.all_to_all(arrived, "row", split_axis=0, concat_axis=1, tiled=True)
+    peers = lax.axis_size("row")
+    pieces = jnp.stack(jnp.split(arrived, peers, axis=0), axis=0)
+    pieces = lax.all_to_all(pieces, "row", split_axis=0, concat_axis=0)
+    arrived = jnp.concatenate(pieces, axis=1)
     left_far, right_far = operands(flatten_normed(arrived), in_weights[1], arrived.shape)
     gating_far = gates(flatten_normed(middle), gate_weights[1], shape)
     return finish(middle, gating_far, triangle(left_far, right_far), out_weights[1])

time: 86.9 us -> 89.6 us (1.031)
  local copies, waits for them, and re-layouts: 6.25 us -> 9.69 us
    unnamed x13 -> x18, local copies, waits for them, and re-layouts: 2.22 us -> 5.68 us
where the time goes in v1:
time: 89.6 us; the launch traced here: 89 us
  blocking collectives  54.7 us (61%)
  local copies, waits for them, and re-layouts  9.69 us (11%)
  waiting for transfers between devices  8.39 us (9%)
  starting transfers between devices  6.58 us (7%)
  matrix products  5.78 us (6%)
  other arithmetic  3 us (3%)
    unnamed x2, blocking collectives  35.7 us
    all_gather x2, blocking collectives, triangle(): lax.all_gather(right_rows, 'row', axis=0, tiled=True)  19 us
    unnamed x18, local copies, waits for them, and re-layouts  5.68 us
    all_to_all x1, waiting for transfers between devices, per_device(): lax.all_to_all(jnp.swapaxes(middle, 0, 1), 'ka', split_axis=1, concat_axi...  4.65 us
    all_to_all x1, waiting for transfers between devices, per_device(): pieces = lax.all_to_all(pieces, 'row', split_axis=0, concat_axis=0)  3.74 us
    all_to_all x1, starting transfers between devices, per_device(): pieces = lax.all_to_all(pieces, 'row', split_axis=0, concat_axis=0)  3.33 us
    all_to_all x1, starting transfers between devices, per_device(): lax.all_to_all(jnp.swapaxes(middle, 0, 1), 'ka', split_axis=1, concat_axi...  3.25 us
    all_gather x2, local copies, waits for them, and re-layouts, triangle(): lax.all_gather(right_rows, 'row', axis=0, tiled=True)  2.86 us
  transfers between devices with their start and end apart: 2, of which 2 were waited for; matrix products, arithmetic and copies ran while one was open for 2% of the time, Pallas kernels for 0%

profile of v1, /device:TPU:0, one launch (start us, length us, event | category | flops | bytes accessed | tf_op | source)
XLA Modules:
  0.0 89.0 jit_solution(16018863513838881642)
XLA Ops:
  0.0 0.9 convert_reduce_fusion.1
  1.0 1.1 %fusion.16 = f32[32,512]{1,0:T(8,128)S(1)} fusion(bf16[2,128,512]{2,1,0:T(8,128)(2,1)} %param.5, bf16[4,8,128]{2,1,0:T(8,128)(2,1)S(1)} %copy-done.1, f32[4,8]{1,0:T(4,128)S(1)} %add_rsqrt_fusion.4, f32[4,8]{1,0:T(4,128)S(1)} %broadcast_multiply_fusion.4), kind=kOutput, calls=%fused_computation.22 | convolution fusion | flops 4210688 | bytes 205056 | tf_op jit(solution)/shard_map/dot_general | solution.py:24
  2.2 10.7 %all_gather.6 = bf16[32,8,128]{2,1,0:T(8,128)(2,1)S(1)} all-gather(bf16[4,8,128]{2,1,0:T(8,128)(2,1)S(1)} %get-tuple-element.8), channel_id=1, replica_groups=mesh['row'=8,'ka'=4] {'row'}, dimensions={0}, use_global_device_ids=true | all-gather | bytes 73728 | tf_op jit(solution)/shard_map/all_gather | solution.py:46
  12.9 1.4 %copy.68 = bf16[32,8,128]{1,0,2:T(8,128)(2,1)S(1)} copy(bf16[32,8,128]{2,1,0:T(8,128)(2,1)S(1)} %all_gather.6) | data formatting | bytes 131072 | tf_op jit(solution)/shard_map/all_gather | solution.py:46
  14.5 0.6 fusion
  15.3 19.4 %all-reduce = bf16[4,32,128]{2,0,1:T(4,128)(2,1)S(1)} all-reduce(bf16[4,32,128]{2,0,1:T(4,128)(2,1)S(1)} %copy.70), channel_id=2, replica_groups=mesh['row'=8,'ka'=4] {'ka'}, use_global_device_ids=true, to_apply=%region_2.0.clone | all-reduce | flops 16384 | bytes 65536
  34.7 0.6 copy-done.4
  35.3 0.6 dynamic-slice
  37.5 0.7 convert_reduce_fusion
  38.3 3.2 %all-to-all-start = ((bf16[8,4,128]{2,0,1:T(8,128)(2,1)}), bf16[8,4,128]{2,0,1:T(8,128)(2,1)S(1)}, u32[]{:S(2)}, u32[]{:S(2)}) async-start(bf16[8,4,128]{2,0,1:T(8,128)(2,1)} %bitcast.12), calls=%async_computation | async-start | bytes 16384 | tf_op jit(solution)/shard_map/all_to_all | solution.py:66
  41.5 0.9 fusion.42
  42.4 4.6 %all-to-all-done = bf16[8,4,128]{2,0,1:T(8,128)(2,1)S(1)} async-done(((bf16[8,4,128]{2,0,1:T(8,128)(2,1)}), bf16[8,4,128]{2,0,1:T(8,128)(2,1)S(1)}, u32[]{:S(2)}, u32[]{:S(2)}) %all-to-all-start) | async-done | bytes 8224 | tf_op jit(solution)/shard_map/all_to_all | solution.py:66
  47.1 0.6 constant_dynamic-update-slice_fusion.7
  47.7 0.6 constant_dynamic-update-slice_fusion.6
  49.4 0.6 constant_dynamic-update-slice_fusion.3
  51.1 0.6 constant_dynamic-update-slice_fusion
  51.7 3.3 %all-to-all-start.1 = ((bf16[8,4,1,128]{3,1,2,0:T(4,128)(2,1)}), bf16[8,4,1,128]{3,1,2,0:T(4,128)(2,1)S(1)}, u32[]{:S(2)}, u32[]{:S(2)}) async-start(bf16[8,4,1,128]{3,1,2,0:T(4,128)(2,1)} %constant_dynamic-update-slice_fusion), calls=%async_computation.1 | async-start | bytes 16384 | tf_op jit(solution)/shard_map/all_to_all | solution.py:71
  55.1 0.9 %fusion.6 = f32[4,8,128]{2,1,0:T(8,128)S(1)} fusion(bf16[2,128,128]{2,1,0:T(8,128)(2,1)S(1)} %copy-done.3, bf16[4,8,128]{2,1,0:T(8,128)(2,1)} %get-tuple-element.10, f32[4,8]{1,0:T(4,128)S(1)} %add_rsqrt_fusion.3, f32[4,8]{1,0:T(4,128)S(1)} %broadcast_multiply_fusion.3), kind=kOutput, calls=%fused_computation.10 | convolution fusion | flops 1077248 | bytes 61440 | tf_op jit(solution)/shard_map/dot_general | solution.py:38
  56.0 3.7 %all-to-all-done.1 = bf16[8,4,1,128]{3,1,2,0:T(4,128)(2,1)S(1)} async-done(((bf16[8,4,1,128]{3,1,2,0:T(4,128)(2,1)}), bf16[8,4,1,128]{3,1,2,0:T(4,128)(2,1)S(1)}, u32[]{:S(2)}, u32[]{:S(2)}) %all-to-all-start.1) | async-done | bytes 8224 | tf_op jit(solution)/shard_map/all_to_all | solution.py:71
  60.2 8.3 %all_gather.7 = bf16[32,8,128]{2,1,0:T(8,128)(2,1)S(1)} all-gather(bf16[4,8,128]{2,1,0:T(8,128)(2,1)S(1)} %get-tuple-element.6), channel_id=1, replica_groups=mesh['row'=8,'ka'=4] {'row'}, dimensions={0}, use_global_device_ids=true | all-gather | bytes 73728 | tf_op jit(solution)/shard_map/all_gather | solution.py:46
  68.5 1.4 %copy.82 = bf16[32,8,128]{1,0,2:T(8,128)(2,1)S(1)} copy(bf16[32,8,128]{2,1,0:T(8,128)(2,1)S(1)} %all_gather.7) | data formatting | bytes 131072 | tf_op jit(solution)/shard_map/all_gather | solution.py:46
  70.1 0.6 fusion.1
  70.9 16.3 %all-reduce.1 = bf16[4,32,128]{2,0,1:T(4,128)(2,1)S(1)} all-reduce(bf16[4,32,128]{2,0,1:T(4,128)(2,1)S(1)} %copy.84), channel_id=3, replica_groups=mesh['row'=8,'ka'=4] {'ka'}, use_global_device_ids=true, to_apply=%region_9.0.clone | all-reduce | flops 16384 | bytes 65536
  87.5 1.4 %fusion.13 = bf16[4,8,128]{2,1,0:T(8,128)(2,1)} fusion(f32[4,8,128]{2,1,0:T(8,128)S(1)} %fusion.6, bf16[2,128,128]{2,1,0:T(8,128)(2,1)S(1)} %copy-done.2, bf16[4,8,128]{2,1,0:T(8,128)(2,1)} %get-tuple-element.10, bf16[4,8,128]{2,0,1:T(4,128)(2,1)S(1)} %fusion.39), kind=kOutput, calls=%fused_computation.19 | convolution fusion | flops 1064960 | bytes 73728 | tf_op jit(solution)/shard_map/dot_general | solution.py:56
  (41 shorter events, 4.8 us)
Async XLA Ops:
  0.0 0.9 copy-start.1
  15.3 21.7 %copy-start.3 = (bf16[2,128,128]{2,1,0:T(8,128)(2,1)S(1)}, bf16[2,128,128]{2,1,0:T(8,128)(2,1)}, u32[]{:S(2)}) copy-start(bf16[2,128,128]{2,1,0:T(8,128)(2,1)} %param.6) | copy-start | bytes 196612
  34.7 0.7 copy-start.4
  36.7 0.8 copy-start.2
  36.8 23.2 %copy-start = (bf16[2,128,512]{2,1,0:T(8,128)(2,1)S(1)}, bf16[2,128,512]{2,1,0:T(8,128)(2,1)}, u32[]{:S(2)}) copy-start(bf16[2,128,512]{2,1,0:T(8,128)(2,1)} %param.5) | copy-start | bytes 786436
  38.3 8.8 %all-to-all-start = ((bf16[8,4,128]{2,0,1:T(8,128)(2,1)}), bf16[8,4,128]{2,0,1:T(8,128)(2,1)S(1)}, u32[]{:S(2)}, u32[]{:S(2)}) async-start(bf16[8,4,128]{2,0,1:T(8,128)(2,1)} %bitcast.12), calls=%async_computation | async-start | bytes 16384 | tf_op jit(solution)/shard_map/all_to_all | solution.py:66
  51.7 8.0 %all-to-all-start.1 = ((bf16[8,4,1,128]{3,1,2,0:T(4,128)(2,1)}), bf16[8,4,1,128]{3,1,2,0:T(4,128)(2,1)S(1)}, u32[]{:S(2)}, u32[]{:S(2)}) async-start(bf16[8,4,1,128]{3,1,2,0:T(4,128)(2,1)} %constant_dynamic-update-slice_fusion), calls=%async_computation.1 | async-start | bytes 16384 | tf_op jit(solution)/shard_map/all_to_all | solution.py:71
